TPU v7x, 256 devices: a whole 4x4x8 slice. The times are simulated.
256 devices in a mesh: prow: 4 (over z_hi, core), pcol: 4 (over y), pl: 16 (over z_lo, x).
Axes of the slice: x: 4, y: 4, z: 8 (z_hi: 2, z_lo: 4; z = z_hi * 4 + z_lo), core: 2. Of those that a mesh axis runs over, the one named last changes fastest.
Arguments:
- factor_cols: bfloat16 [32768, 4096], P(('prow', 'pcol'), 'pl'), may hold values from -0.09375 to 0.09375
- modal_at_loads: bfloat16 [2048, 32768], P(None, ('prow', 'pcol')), may hold values from -0.03125 to 0.03125
- mode_shapes: bfloat16 [8192, 2048], P(('prow', 'pl')), may hold values from -0.125 to 0.125
- natural_freq: float32 [2048], replicated, may hold values from 0.5 to 2
- damping: float32 [2048], replicated, may hold values from 0.05 to 0.2
Outputs:
- cospectrum: float32 [8192, 8192], P(('prow', 'pl'), 'pcol')
All inputs are finite; a program needn't handle non-finite values.
Results may differ from a plain program's by a relative error of at most 0.022.
Values may be sent and summed in bfloat16 or wider, within the bound.
A program may use at most 128 MiB of HBM per device.

v0:
```python
import jax
import jax.numpy as jnp
from jax import lax
from jax.sharding import PartitionSpec as P


def transfer_pair(natural_freq, damping):
    detuning = natural_freq * natural_freq - 1.0
    damper = 2.0 * damping * natural_freq
    modulus = detuning * detuning + damper * damper
    return (detuning / modulus, -damper / modulus)


def outer_rows(left_rows, right_rows):
    return lax.dot_general(
        left_rows, right_rows, (((1,), (1,)), ((), ())), preferred_element_type=jnp.float32
    )


def make_body(n_row, n_col):
    swap = [(c * n_col + r, r * n_col + c) for r in range(n_row) for c in range(n_col)]

    def body(factor_cols, modal_at_loads, mode_shapes, natural_freq, damping):
        in_phase, quadrature = transfer_pair(natural_freq, damping)
        own_rows = lax.psum_scatter(
            jnp.dot(modal_at_loads, factor_cols, preferred_element_type=jnp.float32),
            ("prow", "pcol"),
            scatter_dimension=0,
            tiled=True,
        )
        modal_load = lax.all_gather(
            own_rows.astype(jnp.bfloat16), ("prow", "pcol"), axis=0, tiled=True
        )
        modal_wide = modal_load.astype(jnp.float32)
        pseudo = jnp.concatenate(
            [
                (in_phase[:, None] * modal_wide).astype(jnp.bfloat16),
                (quadrature[:, None] * modal_wide).astype(jnp.bfloat16),
            ],
            axis=1,
        )
        block = pseudo.shape[0] // (n_row * n_col)
        row, col = (lax.axis_index("prow"), lax.axis_index("pcol"))
        first_row = (col * n_row + row) * block
        own_pseudo = lax.dynamic_slice_in_dim(pseudo, first_row, block, 0)
        partial_gram = outer_rows(own_pseudo, pseudo)
        gram_block = lax.psum(partial_gram.astype(jnp.bfloat16), "pl")
        gram_panel = lax.all_gather(gram_block, "prow", axis=0, tiled=True)
        weighted_part = outer_rows(mode_shapes, gram_panel).astype(jnp.bfloat16)
        weighted = lax.all_gather(weighted_part, "pcol", axis=1, tiled=True)
        panel_piece = lax.ppermute(mode_shapes, ("prow", "pcol"), swap)
        return outer_rows(weighted, lax.all_gather(panel_piece, "pl", axis=0, tiled=True))

    return body


def solution(mesh):
    in_specs = (
        P(("prow", "pcol"), "pl"),
        P(None, ("prow", "pcol")),
        P(("prow", "pl"), None),
        P(),
        P(),
    )
    out_specs = P(("prow", "pl"), "pcol")
    body = make_body(mesh.shape["prow"], mesh.shape["pcol"])
    return jax.shard_map(body, mesh=mesh, in_specs=in_specs, out_specs=out_specs, check_vma=False)
```

profile of v0, /device:TPU:1, one launch (start us, length us, event | category | flops | bytes accessed | tf_op | source)
XLA Modules:
  0.0 488.3 jit_solution(12734103664353830712)
XLA Ops:
  6.5 1.2 copy-done
  7.8 7.1 %fusion.8 = f32[2048,256]{1,0:T(8,128)} fusion(bf16[2048,2048]{1,0:T(8,128)(2,1)} %param.6, bf16[2048,256]{1,0:T(8,128)(2,1)S(1)} %copy-done), kind=kOutput, calls=%fused_computation.18 | convolution fusion | flops 2147483648 | bytes 11534336 | tf_op jit(solution)/shard_map/dot_general | solution.py:26
  14.8 0.0 reduce-scatter.2.cloned.1.call-update
  14.9 0.0 all-gather.4.cloned.1.call-start
  14.9 90.0 %reduce-scatter.2.cloned.1.call-done = f32[128,256]{1,0:T(8,128)} async-done(((f32[2048,256]{1,0:T(8,128)}), f32[128,256]{1,0:T(8,128)}) %reduce-scatter.2.cloned.1.call-update) | async-done | bytes 131088 | tf_op jit(solution)/shard_map/reduce_scatter | solution.py:25
  104.9 1.5 convert_element_type.21
  106.5 0.0 all-gather.4.cloned.1.call-update
  106.5 0.0 all-reduce.2.cloned.1.call-start
  106.6 54.7 %all-gather.4.cloned.1.call-done = bf16[2048,256]{1,0:T(8,128)(2,1)} async-done(((bf16[128,256]{1,0:T(8,128)(2,1)}), bf16[2048,256]{1,0:T(8,128)(2,1)}) %all-gather.4.cloned.1.call-update) | async-done | bytes 1048592 | tf_op jit(solution)/shard_map/all_gather | solution.py:31
  161.3 1.8 fusion
  163.1 1.6 convolution_convert_fusion
  164.7 0.0 all-reduce.2.cloned.1.call-update
  164.7 0.0 all-gather.6.cloned.1.call-start
  164.7 146.3 %all-reduce.2.cloned.1.call-done = bf16[128,2048]{1,0:T(8,128)(2,1)} async-done(((bf16[128,2048]{1,0:T(8,128)(2,1)}), bf16[128,2048]{1,0:T(8,128)(2,1)}) %all-reduce.2.cloned.1.call-update) | async-done | bytes 524304 | tf_op jit(solution)/shard_map/psum | solution.py:47
  311.1 0.0 all-gather.6.cloned.1.call-update
  311.1 0.0 all-gather.8.cloned.1.call-start
  311.1 14.3 %collective-permute-start = (bf16[128,2048]{1,0:T(8,128)(2,1)S(1)}, bf16[128,2048]{1,0:T(8,128)(2,1)S(1)}, u32[]{:S(2)}, u32[]{:S(2)}) collective-permute-start(bf16[128,2048]{1,0:T(8,128)(2,1)S(1)} %copy-done.2), channel_id=1, source_target_pairs={{0,0},{64,16},{128,32},{192,48},{16,64},{80,80},{144,96},{208,112}... | collective-permute-start | bytes 1572872 | tf_op jit(solution)/shard_map/ppermute | solution.py:51
  325.4 7.8 %collective-permute-done = bf16[128,2048]{1,0:T(8,128)(2,1)S(1)} collective-permute-done((bf16[128,2048]{1,0:T(8,128)(2,1)S(1)}, bf16[128,2048]{1,0:T(8,128)(2,1)S(1)}, u32[]{:S(2)}, u32[]{:S(2)}) %collective-permute-start) | collective-permute-done | bytes 524320 | tf_op jit(solution)/shard_map/ppermute | solution.py:51
  333.2 0.8 copy-done.1
  334.1 34.2 %all-gather.6.cloned.1.call-done = bf16[512,2048]{1,0:T(8,128)(2,1)} async-done(((bf16[128,2048]{1,0:T(8,128)(2,1)}), bf16[512,2048]{1,0:T(8,128)(2,1)}) %all-gather.6.cloned.1.call-update) | async-done | bytes 2097168 | tf_op jit(solution)/shard_map/all_gather | solution.py:48
  368.3 2.3 fusion.2
  370.6 9.9 %all_gather.14 = bf16[128,2048]{0,1:T(8,128)(2,1)S(1)} all-gather(bf16[128,512]{0,1:T(8,128)(2,1)S(1)} %fusion.2), channel_id=1, replica_groups=mesh['prow'=4,'pcol'=4,'pl'=16] {'pcol'}, dimensions={1}, use_global_device_ids=true | all-gather | bytes 655360 | tf_op jit(solution)/shard_map/all_gather | solution.py:50
  380.5 94.0 %all-gather.8.cloned.1.call-done = bf16[2048,2048]{1,0:T(8,128)(2,1)} async-done(((bf16[128,2048]{1,0:T(8,128)(2,1)}), bf16[2048,2048]{1,0:T(8,128)(2,1)}) %all-gather.8.cloned.1.call-update) | async-done | bytes 8388624 | tf_op jit(solution)/shard_map/all_gather | solution.py:52
  474.5 7.3 %fusion.9 = f32[128,2048]{1,0:T(8,128)} fusion(bf16[128,2048]{0,1:T(8,128)(2,1)S(1)} %all_gather.14, bf16[2048,2048]{1,0:T(8,128)(2,1)} %all-gather.8.cloned.1.call-done), kind=kOutput, calls=%fused_computation.19 | convolution fusion | flops 1073741824 | bytes 9961472 | tf_op jit(solution)/shard_map/dot_general | solution.py:15
  (11 shorter events, 0.0 us)
Async XLA Ops:
  6.5 1.2 copy-start
  6.5 98.4 %reduce-scatter.2.cloned.1.call-start = ((), (), s32[]{:S(2)}) async-start(), calls=%async_computation.1 | async-start | bytes 2228224 | tf_op jit(solution)/shard_map/reduce_scatter | solution.py:25
  14.8 91.7 %copy-start.3 = (f32[2048]{0:T(1024)S(1)}, f32[2048]{0:T(1024)}, u32[]{:S(2)}) copy-start(f32[2048]{0:T(1024)} %param.8) | copy-start | bytes 24580
  14.8 91.7 %copy-start.4 = (f32[2048]{0:T(1024)S(1)}, f32[2048]{0:T(1024)}, u32[]{:S(2)}) copy-start(f32[2048]{0:T(1024)} %param.9) | copy-start | bytes 24580
  14.9 146.4 %all-gather.4.cloned.1.call-start = ((), (), s32[]{:S(2)}) async-start(), calls=%async_computation.2 | async-start | bytes 1114112 | tf_op jit(solution)/shard_map/all_gather | solution.py:31
  106.5 204.6 %all-reduce.2.cloned.1.call-start = ((), (), s32[]{:S(2)}) async-start(), calls=%async_computation.3 | async-start | bytes 1048576 | tf_op jit(solution)/shard_map/psum | solution.py:47
  163.0 148.1 %copy-start.2 = (bf16[128,2048]{1,0:T(8,128)(2,1)S(1)}, bf16[128,2048]{1,0:T(8,128)(2,1)}, u32[]{:S(2)}) copy-start(bf16[128,2048]{1,0:T(8,128)(2,1)} %param.7) | copy-start | bytes 1572868
  164.7 203.6 %all-gather.6.cloned.1.call-start = ((), (), s32[]{:S(2)}) async-start(), calls=%async_computation.4 | async-start | bytes 2621440 | tf_op jit(solution)/shard_map/all_gather | solution.py:48
  311.1 163.4 %all-gather.8.cloned.1.call-start = ((), (), s32[]{:S(2)}) async-start(), calls=%async_computation.5 | async-start | bytes 8912896 | tf_op jit(solution)/shard_map/all_gather | solution.py:52
  311.1 22.1 %collective-permute-start = (bf16[128,2048]{1,0:T(8,128)(2,1)S(1)}, bf16[128,2048]{1,0:T(8,128)(2,1)S(1)}, u32[]{:S(2)}, u32[]{:S(2)}) collective-permute-start(bf16[128,2048]{1,0:T(8,128)(2,1)S(1)} %copy-done.2), channel_id=1, source_target_pairs={{0,0},{64,16},{128,32},{192,48},{16,64},{80,80},{144,96},{208,112}... | collective-permute-start | bytes 1572872 | tf_op jit(solution)/shard_map/ppermute | solution.py:51
  333.2 0.8 copy-start.1
Sparse Core Ops, SparseCore 0:
  15.0 89.8 reduce-scatter.1
  107.7 53.5 all-gather.3
  164.8 146.2 all-reduce.1
  312.9 55.3 all-gather.5
  370.1 104.3 all-gather.7
where the time goes:
time: 489 us; the launch traced here: 488 us
  waiting for transfers between devices  427 us (87%)
  matrix products  18.3 us (4%)
  starting transfers between devices  14.5 us (3%)
  between operations  13.2 us (3%)
  blocking collectives  9.9 us (2%)
    psum x1, waiting for transfers between devices, body(): gram_block = lax.psum(partial_gram.astype(jnp.bfloat16), 'pl')  146 us
    all_gather x1, waiting for transfers between devices, body(): lax.all_gather(panel_piece, 'pl', axis=0, tiled=True)  94 us
    reduce_scatter x1, waiting for transfers between devices, body(): lax.psum_scatter(jnp.dot(modal_at_loads, factor_cols, preferred_element_t...  90 us
    all_gather x1, waiting for transfers between devices, body(): lax.all_gather(own_rows.astype(jnp.bfloat16), ('prow', 'pcol'), axis=0, t...  54.7 us
    all_gather x1, waiting for transfers between devices, body(): gram_panel = lax.all_gather(gram_block, 'prow', axis=0, tiled=True)  34.2 us
    ppermute x1, starting transfers between devices, body(): panel_piece = lax.ppermute(mode_shapes, ('prow', 'pcol'), swap)  14.3 us
    dot_general x3, matrix products, outer_rows(): lax.dot_general(left_rows, right_rows, (((1,), (1,)), ((), ())), preferre...  11.2 us
    all_gather x1, blocking collectives, body(): weighted = lax.all_gather(weighted_part, 'pcol', axis=1, tiled=True)  9.9 us
  transfers between devices with their start and end apart: 6, of which 6 were waited for; matrix products, arithmetic and copies ran while one was open for 0% of the time, Pallas kernels for 0%

commit v1 on v0

--- a/solution.py
+++ b/solution.py
@@ -44,7 +44,7 @@
         first_row = (col * n_row + row) * block
         own_pseudo = lax.dynamic_slice_in_dim(pseudo, first_row, block, 0)
         partial_gram = outer_rows(own_pseudo, pseudo)
-        gram_block = lax.psum(partial_gram.astype(jnp.bfloat16), "pl")
+        gram_block = jnp.sum(lax.all_gather(partial_gram.astype(jnp.bfloat16), "pl"), axis=0)
         gram_panel = lax.all_gather(gram_block, "prow", axis=0, tiled=True)
         weighted_part = outer_rows(mode_shapes, gram_panel).astype(jnp.bfloat16)
         weighted = lax.all_gather(weighted_part, "pcol", axis=1, tiled=True)

time: 489 us -> 438 us (0.90)
  waiting for transfers between devices: 427 us -> 381 us
  starting transfers between devices: 14.5 us -> 3.84 us
  other arithmetic: 3.3 us -> 9.49 us
    psum x1 -> x0, waiting for transfers between devices: 146 us -> none  [body(): gram_block = lax.psum(partial_gram.astype(jnp.bfloat16), 'pl')]
    all_gather x0 -> x1, waiting for transfers between devices: none -> 97.7 us  [body(): lax.all_gather(partial_gram.astype(jnp.bfloat16), 'pl')]
    ppermute x1, starting transfers between devices: 14.3 us -> 3.67 us  [body(): panel_piece = lax.ppermute(mode_shapes, ('prow', 'pcol'), swap)]
    reduce_sum x0 -> x1, other arithmetic: none -> 6.19 us  [body(): jnp.sum(lax.all_gather(partial_gram.astype(jnp.bfloat16), 'pl'), axis=0)]
  transfers between devices with their start and end apart: 6 -> 6, of which waited for: 6 -> 6; matrix products, arithmetic and copies ran while one was open for 0% -> 1% of each run, Pallas kernels for 0% -> 0%
where the time goes in v1:
time: 438 us
  waiting for transfers between devices  381 us (87%)
  matrix products  18.3 us (4%)
  between operations  13.2 us (3%)
  blocking collectives  9.9 us (2%)
  other arithmetic  9.49 us (2%)
    all_gather x1, waiting for transfers between devices, body(): lax.all_gather(partial_gram.astype(jnp.bfloat16), 'pl')  97.7 us
    all_gather x1, waiting for transfers between devices, body(): lax.all_gather(panel_piece, 'pl', axis=0, tiled=True)  96.3 us
    reduce_scatter x1, waiting for transfers between devices, body(): lax.psum_scatter(jnp.dot(modal_at_loads, factor_cols, preferred_element_t...  90 us
    all_gather x1, waiting for transfers between devices, body(): lax.all_gather(own_rows.astype(jnp.bfloat16), ('prow', 'pcol'), axis=0, t...  54.7 us
    all_gather x1, waiting for transfers between devices, body(): gram_panel = lax.all_gather(gram_block, 'prow', axis=0, tiled=True)  35.4 us
    dot_general x3, matrix products, outer_rows(): lax.dot_general(left_rows, right_rows, (((1,), (1,)), ((), ())), preferre...  11.2 us
    all_gather x1, blocking collectives, body(): weighted = lax.all_gather(weighted_part, 'pcol', axis=1, tiled=True)  9.9 us
  transfers between devices with their start and end apart: 6, of which 6 were waited for; matrix products, arithmetic and copies ran while one was open for 1% of the time, Pallas kernels for 0%

profile of v1, /device:TPU:1, one launch (start us, length us, event | category | flops | bytes accessed | tf_op | source)
XLA Modules:
  0.0 437.8 jit_solution(12797681611252640683)
XLA Ops:
  6.5 1.2 copy-done
  7.8 7.1 %fusion.8 = f32[2048,256]{1,0:T(8,128)} fusion(bf16[2048,2048]{1,0:T(8,128)(2,1)} %param.6, bf16[2048,256]{1,0:T(8,128)(2,1)S(1)} %copy-done), kind=kOutput, calls=%fused_computation.18 | convolution fusion | flops 2147483648 | bytes 11534336 | tf_op jit(solution)/shard_map/dot_general | solution.py:26
  14.8 0.0 reduce-scatter.2.cloned.1.call-update
  14.9 0.0 all-gather.6.cloned.1.call-start
  14.9 90.0 %reduce-scatter.2.cloned.1.call-done = f32[128,256]{1,0:T(8,128)} async-done(((f32[2048,256]{1,0:T(8,128)}), f32[128,256]{1,0:T(8,128)}) %reduce-scatter.2.cloned.1.call-update) | async-done | bytes 131088 | tf_op jit(solution)/shard_map/reduce_scatter | solution.py:25
  104.9 1.5 convert_element_type.23
  106.5 0.0 all-gather.6.cloned.1.call-update
  106.5 0.0 all-gather.12.cloned.1.call-start
  106.6 54.7 %all-gather.6.cloned.1.call-done = bf16[2048,256]{1,0:T(8,128)(2,1)} async-done(((bf16[128,256]{1,0:T(8,128)(2,1)}), bf16[2048,256]{1,0:T(8,128)(2,1)}) %all-gather.6.cloned.1.call-update) | async-done | bytes 1048592 | tf_op jit(solution)/shard_map/all_gather | solution.py:31
  161.3 1.8 fusion
  163.0 1.6 convolution_convert_fusion
  164.6 0.0 all-gather.12.cloned.1.call-update
  164.7 0.0 all-gather.8.cloned.1.call-start
  164.7 97.7 %all-gather.12.cloned.1.call-done = bf16[2048,2048]{1,0:T(8,128)(2,1)} async-done(((bf16[128,2048]{1,0:T(8,128)(2,1)}), bf16[2048,2048]{1,0:T(8,128)(2,1)}) %all-gather.12.cloned.1.call-update) | async-done | bytes 8388624 | tf_op jit(solution)/shard_map/all_gather | solution.py:47
  262.5 6.2 %reduce_sum.12 = bf16[128,2048]{1,0:T(8,128)(2,1)} reduce(bf16[16,128,2048]{2,1,0:T(8,128)(2,1)} %bitcast.9, bf16[]{:T(256)} %constant.25.clone.1), dimensions={0}, to_apply=%region_1.0 | reduce | flops 3932160 | bytes 8912898 | tf_op jit(solution)/shard_map/reduce_sum | solution.py:47
  268.7 0.0 all-gather.10.cloned.1.call-start
  268.7 3.7 collective-permute-start
  272.4 6.8 %collective-permute-done = bf16[128,2048]{1,0:T(8,128)(2,1)S(1)} collective-permute-done((bf16[128,2048]{1,0:T(8,128)(2,1)S(1)}, bf16[128,2048]{1,0:T(8,128)(2,1)S(1)}, u32[]{:S(2)}, u32[]{:S(2)}) %collective-permute-start) | collective-permute-done | bytes 524320 | tf_op jit(solution)/shard_map/ppermute | solution.py:51
  279.3 0.8 copy-done.1
  280.1 35.4 %all-gather.8.cloned.1.call-done = bf16[512,2048]{1,0:T(8,128)(2,1)} async-done(((bf16[128,2048]{1,0:T(8,128)(2,1)}), bf16[512,2048]{1,0:T(8,128)(2,1)}) %all-gather.8.cloned.1.call-update) | async-done | bytes 2097168 | tf_op jit(solution)/shard_map/all_gather | solution.py:48
  315.5 2.3 fusion.2
  317.8 9.9 %all_gather.22 = bf16[128,2048]{0,1:T(8,128)(2,1)S(1)} all-gather(bf16[128,512]{0,1:T(8,128)(2,1)S(1)} %fusion.2), channel_id=1, replica_groups=mesh['prow'=4,'pcol'=4,'pl'=16] {'pcol'}, dimensions={1}, use_global_device_ids=true | all-gather | bytes 655360 | tf_op jit(solution)/shard_map/all_gather | solution.py:50
  327.7 96.3 %all-gather.10.cloned.1.call-done = bf16[2048,2048]{1,0:T(8,128)(2,1)} async-done(((bf16[128,2048]{1,0:T(8,128)(2,1)}), bf16[2048,2048]{1,0:T(8,128)(2,1)}) %all-gather.10.cloned.1.call-update) | async-done | bytes 8388624 | tf_op jit(solution)/shard_map/all_gather | solution.py:52
  424.0 7.3 %fusion.9 = f32[128,2048]{1,0:T(8,128)} fusion(bf16[128,2048]{0,1:T(8,128)(2,1)S(1)} %all_gather.22, bf16[2048,2048]{1,0:T(8,128)(2,1)} %all-gather.10.cloned.1.call-done), kind=kOutput, calls=%fused_computation.19 | convolution fusion | flops 1073741824 | bytes 9961472 | tf_op jit(solution)/shard_map/dot_general | solution.py:15
  (12 shorter events, 0.1 us)
Async XLA Ops:
  6.5 1.2 copy-start
  6.5 98.4 %reduce-scatter.2.cloned.1.call-start = ((), (), s32[]{:S(2)}) async-start(), calls=%async_computation.1 | async-start | bytes 2228224 | tf_op jit(solution)/shard_map/reduce_scatter | solution.py:25
  14.8 91.7 %copy-start.3 = (f32[2048]{0:T(1024)S(1)}, f32[2048]{0:T(1024)}, u32[]{:S(2)}) copy-start(f32[2048]{0:T(1024)} %param.8) | copy-start | bytes 24580
  14.8 91.7 %copy-start.4 = (f32[2048]{0:T(1024)S(1)}, f32[2048]{0:T(1024)}, u32[]{:S(2)}) copy-start(f32[2048]{0:T(1024)} %param.9) | copy-start | bytes 24580
  14.9 146.4 %all-gather.6.cloned.1.call-start = ((), (), s32[]{:S(2)}) async-start(), calls=%async_computation.2 | async-start | bytes 1114112 | tf_op jit(solution)/shard_map/all_gather | solution.py:31
  106.5 156.0 %all-gather.12.cloned.1.call-start = ((), (), s32[]{:S(2)}) async-start(), calls=%async_computation.5 | async-start | bytes 8912896 | tf_op jit(solution)/shard_map/all_gather | solution.py:47
  164.7 150.8 %all-gather.8.cloned.1.call-start = ((), (), s32[]{:S(2)}) async-start(), calls=%async_computation.3 | async-start | bytes 2621440 | tf_op jit(solution)/shard_map/all_gather | solution.py:48
  262.5 6.3 %copy-start.2 = (bf16[128,2048]{1,0:T(8,128)(2,1)S(1)}, bf16[128,2048]{1,0:T(8,128)(2,1)}, u32[]{:S(2)}) copy-start(bf16[128,2048]{1,0:T(8,128)(2,1)} %param.7) | copy-start | bytes 1572868
  268.7 155.4 %all-gather.10.cloned.1.call-start = ((), (), s32[]{:S(2)}) async-start(), calls=%async_computation.4 | async-start | bytes 8912896 | tf_op jit(solution)/shard_map/all_gather | solution.py:52
  268.7 10.5 %collective-permute-start = (bf16[128,2048]{1,0:T(8,128)(2,1)S(1)}, bf16[128,2048]{1,0:T(8,128)(2,1)S(1)}, u32[]{:S(2)}, u32[]{:S(2)}) collective-permute-start(bf16[128,2048]{1,0:T(8,128)(2,1)S(1)} %copy-done.2), channel_id=1, source_target_pairs={{0,0},{64,16},{128,32},{192,48},{16,64},{80,80},{144,96},{208,112}... | collective-permute-start | bytes 1572872 | tf_op jit(solution)/shard_map/ppermute | solution.py:51
  279.3 0.8 copy-start.1
Sparse Core Ops, SparseCore 0:
  15.0 89.8 reduce-scatter.1
  107.7 53.5 all-gather.5
  164.8 97.6 all-gather.11
  268.8 46.6 all-gather.7
  317.1 106.8 all-gather.9
